TPU v7x, 32 devices: a whole 2x2x4 slice. The times are simulated.
32 devices in a mesh: ctx: 16 (over z, x, core), ch: 2 (over y).
Axes of the slice: x: 2, y: 2, z: 4, core: 2. Of those that a mesh axis runs over, the one named last changes fastest.
Arguments:
- inputs: bfloat16 [8192, 4096], P('ctx', 'ch'), may hold values from -6 to 6
- proj_weight: bfloat16 [2, 4096, 128], P(None, 'ch'), may hold values from -0.09375 to 0.09375
- filters: float32 [128, 8192], P('ch', 'ctx'), may hold values from -1.5 to 1.5
- skip_gain: float32 [128], P('ch'), may hold values from 0.3 to 1.7
- targets: float32 [128, 8192], P('ch', 'ctx'), may hold values from -6 to 6
Outputs:
- outputs: float32 [128, 8192], P('ch', 'ctx')
- grad_inputs: float32 [8192, 4096], P('ctx', 'ch')
- grad_filter: float32 [128, 8192], P('ch', 'ctx')
- grad_proj: float32 [256, 4096], P('ctx', 'ch')
All inputs are finite; a program needn't handle non-finite values.
Results may differ from a plain program's by a relative error of at most 0.0005.
Values sent between devices are 32-bit elements; how exact they have to be, the bound alone decides.
A program may use at most 64 MiB of HBM per device.

v0:
```python
import math

import functools

import jax
import jax.numpy as jnp
import numpy as np
from jax import lax
from jax.experimental import pallas as pl
from jax.experimental.pallas import tpu as pltpu
from jax.sharding import PartitionSpec as P

HIGHEST = lax.Precision.HIGHEST


def product(left, right):
    return jnp.dot(left, right, precision=HIGHEST, preferred_element_type=jnp.float32)


def angle_table(row_total, col_total, period):
    row_index = lax.broadcasted_iota(jnp.int32, (row_total, col_total), 0)
    col_index = lax.broadcasted_iota(jnp.int32, (row_total, col_total), 1)
    phase_index = row_index * col_index % period
    angles = 2.0 * math.pi / period * phase_index.astype(jnp.float32)
    return (jnp.cos(angles), jnp.sin(angles), row_index, col_index)


def twiddle(real_part, imag_part, frequencies, padded, direction):
    frames = real_part.shape[-1]
    offsets = lax.broadcasted_iota(jnp.int32, (2, frames), 1)
    phase_index = frequencies[:, None] * offsets % padded
    angles = direction * 2.0 * math.pi / padded * phase_index.astype(jnp.float32)
    cosine = jnp.cos(angles)[:, None, None, :]
    sine_table = jnp.sin(angles)[:, None, None, :]
    return (
        real_part * cosine - imag_part * sine_table,
        real_part * sine_table + imag_part * cosine,
    )


def multiply(left_real, left_imag, right_real, right_imag, conj_sign):
    right_imag = conj_sign * right_imag
    return (
        left_real * right_real - left_imag * right_imag,
        left_real * right_imag + left_imag * right_real,
    )


def to_blocks(fields_seq):
    return lax.all_to_all(fields_seq[None], "ctx", split_axis=3, concat_axis=0, tiled=True)


def to_frames(block_grouped):
    return lax.all_to_all(block_grouped, "ctx", split_axis=0, concat_axis=3, tiled=True)[0]


def forward_spectra(block_grouped, cos_big, sin_big, position):
    groups = block_grouped.shape[0]
    fields = block_grouped.shape[1]
    own_channels = block_grouped.shape[2]
    per_peer = block_grouped.shape[3]
    frames = groups * per_peer
    padded = 2 * frames * groups
    flat_layout = block_grouped.reshape(groups, fields * own_channels * per_peer)
    cosine, sine_table, row_index, col_index = angle_table(groups, groups, 2 * groups)
    parity = jnp.where(col_index % 2 == 0, 1.0, -1.0)
    imag_table = jnp.where(row_index == 0, parity, -sine_table)
    payload = jnp.stack([product(cosine, flat_layout), product(imag_table, flat_layout)], 1)
    payload = payload.reshape(payload.shape[0], 2, fields, own_channels, per_peer)
    received = lax.all_to_all(payload, "ctx", split_axis=0, concat_axis=4, tiled=True)
    is_zero = position == 0
    real_first = received[0, 0]
    imag_first = received[0, 1]
    real_part = jnp.stack([real_first, jnp.where(is_zero, imag_first, real_first)])
    imag_part = jnp.stack(
        [jnp.where(is_zero, 0.0, imag_first), jnp.where(is_zero, 0.0, -imag_first)]
    )
    frequencies = jnp.stack([position, jnp.where(is_zero, groups, 2 * groups - position)])
    real_part, imag_part = twiddle(real_part, imag_part, frequencies, padded, -1.0)
    rows_real = real_part.reshape(-1, frames)
    rows_imag = imag_part.reshape(-1, frames)
    out_real = product(rows_real, cos_big) + product(rows_imag, sin_big)
    out_imag = product(rows_imag, cos_big) - product(rows_real, sin_big)
    return (out_real.reshape(real_part.shape), out_imag.reshape(real_part.shape), frequencies)


def invert(real_spec, imag_spec, frequencies, cos_big, sin_big, groups, position):
    spec_shape = real_spec.shape
    fields = spec_shape[1]
    own_channels = spec_shape[2]
    frames = spec_shape[3]
    per_peer = frames // groups
    padded = 2 * frames * groups
    rows_real = real_spec.reshape(-1, frames)
    rows_imag = imag_spec.reshape(-1, frames)
    back_real = product(rows_real, cos_big) - product(rows_imag, sin_big)
    back_imag = product(rows_imag, cos_big) + product(rows_real, sin_big)
    back_real, back_imag = twiddle(
        back_real.reshape(spec_shape), back_imag.reshape(spec_shape), frequencies, padded, 1.0
    )
    is_zero = position == 0
    payload = jnp.stack([back_real[0], jnp.where(is_zero, back_real[1], back_imag[0])])[None]
    received = lax.all_to_all(payload, "ctx", split_axis=4, concat_axis=0, tiled=True)
    slot_count = received.shape[0]
    real_rows = received[:, 0].reshape(slot_count, fields * own_channels * per_peer)
    imag_rows = received[:, 1].reshape(slot_count, fields * own_channels * per_peer)
    cosine, sine_table, row_index, col_index = angle_table(groups, groups, 2 * groups)
    parity = jnp.where(row_index % 2 == 0, 1.0, -1.0)
    real_table = jnp.where(col_index == 0, 1.0, 2.0 * cosine)
    imag_table = jnp.where(col_index == 0, -parity, 2.0 * sine_table)
    result = (product(real_table, real_rows) - product(imag_table, imag_rows)) * (1.0 / padded)
    return result.reshape(groups, fields, own_channels, per_peer)


def general(inputs, proj_weight, filters, skip_gain, targets):
    frames = inputs.shape[0]
    columns = inputs.shape[1]
    channels = proj_weight.shape[2]
    groups = lax.axis_size("ctx")
    position = lax.axis_index("ctx")
    scaling = float(frames * groups) ** (-0.5)
    weight_cols = proj_weight
    projected = lax.psum_scatter(
        jnp.einsum("td,pdc->cpt", inputs, weight_cols, preferred_element_type=jnp.float32),
        "ch",
        scatter_dimension=0,
        tiled=True,
    )
    values = projected[:, 0]
    gates = projected[:, 1]
    cos_big, sin_big, row_index, col_index = angle_table(frames, frames, frames)
    skip_rows = skip_gain[:, None]
    block_grouped = to_blocks(jnp.stack([values, filters]))
    spec_real, spec_imag, frequencies = forward_spectra(block_grouped, cos_big, sin_big, position)
    conv_real, conv_imag = multiply(
        spec_real[:, 0], spec_imag[:, 0], spec_real[:, 1], spec_imag[:, 1], 1.0
    )
    conv_blocks = invert(
        conv_real[:, None], conv_imag[:, None], frequencies, cos_big, sin_big, groups, position
    )
    conv = to_frames(conv_blocks)[0] + skip_rows * values
    outputs_seq = gates * conv
    residual = outputs_seq - targets
    grad_conv = residual * gates
    grad_gate_seq = residual * conv
    grad_blocks = to_blocks(grad_conv[None])
    grad_real, grad_imag, frequencies = forward_spectra(grad_blocks, cos_big, sin_big, position)
    value_real, value_imag = multiply(
        grad_real[:, 0], grad_imag[:, 0], spec_real[:, 1], spec_imag[:, 1], -1.0
    )
    filt_real, filt_imag = multiply(
        grad_real[:, 0], grad_imag[:, 0], spec_real[:, 0], spec_imag[:, 0], -1.0
    )
    returned = invert(
        jnp.stack([value_real, filt_real], 1),
        jnp.stack([value_imag, filt_imag], 1),
        frequencies,
        cos_big,
        sin_big,
        groups,
        position,
    )
    returned_seq = to_frames(returned)
    grad_value_seq = returned_seq[0] + skip_rows * grad_conv
    grad_filter = returned_seq[1]
    grad_pair = jnp.stack([grad_value_seq, grad_gate_seq])
    inputs_wide = inputs.astype(jnp.float32)
    weight_wide = proj_weight.astype(jnp.float32)
    portion = lax.all_gather(grad_pair, "ch", axis=1, tiled=True)
    weight_cols = weight_wide
    summed_in = jnp.einsum(
        "pct,pdc->td", portion, weight_cols, precision=HIGHEST, preferred_element_type=jnp.float32
    )
    block_rows = jnp.einsum(
        "pct,td->pcd", portion, inputs_wide, precision=HIGHEST, preferred_element_type=jnp.float32
    )
    weight_rows = block_rows
    grad_inputs, weight_rows = (summed_in, weight_rows)
    grad_proj = (
        lax.psum_scatter(
            weight_rows.reshape(2 * channels, columns), "ctx", scatter_dimension=0, tiled=True
        )
        * scaling
    )
    return (outputs_seq, grad_inputs, grad_filter * scaling, grad_proj)


MESH = pl.DeviceIdType.MESH
LANES = 128
PIECES = 8
BITES = 2
VMEM_SPEC = pl.BlockSpec(memory_space=pltpu.VMEM)


def exact_dot(left, right):
    return jnp.dot(left, right, precision=HIGHEST, preferred_element_type=jnp.float32)


def spectrum_tables(coarse, fine):
    total = 2 * coarse * fine
    half_shifted = np.arange(coarse)[:, None] + 0.5
    first = 2.0 * np.pi * half_shifted * np.arange(coarse)[None, :] / (2 * coarse)
    middle = 2.0 * np.pi * half_shifted * np.arange(fine)[None, :] / total
    last = 2.0 * np.pi * (np.outer(np.arange(fine), np.arange(fine)) % fine) / fine
    cosine, sine = np.cos(last), np.sin(last)
    return (
        np.concatenate([np.cos(first), -np.sin(first)], 0),
        np.stack([np.cos(middle), -np.sin(middle)]),
        np.block([[cosine, -sine], [sine, cosine]]),
        np.block([[cosine, sine], [-sine, cosine]]),
        np.concatenate([np.cos(first.T), -np.sin(first.T)], 1) * (2.0 / total),
    )


def split(array):
    high = array.astype(jnp.bfloat16)
    return high, (array - high.astype(jnp.float32)).astype(jnp.bfloat16)


def main_kernel(
    own, scaling,
    x_ref, w_ref, filters_ref, targets_ref, skip_ref, t1_ref, mid_ref, t2_ref, t2i_ref, t1i_ref,
    outputs_ref, filter_ref, pair_ref, proj_ref,
    fixed, fixed_in, halves_out, halves_in, fields, fields_in, back_out, back_in,
    part, in1, sum1, in2, sum2, in3,
    fixed_s, fixed_g, half_s, half_g, field_s, field_g, back_s, back_g, relay_s, relay_g,
    s1, g1, s2, g2, s3, g3,
):
    groups, frames = fixed.shape[0], fixed.shape[2]
    columns = x_ref.shape[1]
    splits = frames // LANES
    coarse = groups * splits
    bite = frames // BITES
    channels = 2 * groups * own
    far = groups // 4
    c, h = lax.axis_index("ctx"), lax.axis_index("ch")
    core, x_side, z = lax.rem(c, 2), lax.rem(c // 2, 2), c // 4
    core_peer = c + 1 - 2 * core
    x_peer = c + 2 - 4 * x_side
    z_peers = [lax.rem(c + 4 * d, groups) for d in range(1, far)]
    peers = [lax.rem(c + k, groups) for k in range(1, groups)]
    sources = [lax.rem(c + groups - k, groups) for k in range(1, groups)]
    sent = []

    def send(source, target, send_sem, recv_sem, peer_c, peer_h):
        copy = pltpu.make_async_remote_copy(
            src_ref=source,
            dst_ref=target,
            send_sem=send_sem,
            recv_sem=recv_sem,
            device_id=(peer_c, peer_h),
            device_id_type=MESH,
        )
        copy.start()
        sent.append(copy)
        return copy

    barrier = pltpu.get_barrier_semaphore()
    for peer in peers:
        pl.semaphore_signal(barrier, inc=1, device_id=(peer, h), device_id_type=MESH)
    pl.semaphore_signal(barrier, inc=1, device_id=(c, 1 - h), device_id_type=MESH)

    for g in range(groups):
        fixed[g, :own, :] = filters_ref[g * own : (g + 1) * own, :]
        fixed[g, own:, :] = targets_ref[g * own : (g + 1) * own, :]

    def project(q):
        for p in range(2):
            rows = jnp.dot(
                x_ref[q * bite : (q + 1) * bite, :], w_ref[p], preferred_element_type=jnp.float32
            ).T
            for k in range(2 * groups):
                halves_out[q, k // groups, k % groups, p * own : (p + 1) * own, :] = rows[
                    k * own : (k + 1) * own, :
                ]

    project(0)
    pl.semaphore_wait(barrier, groups)
    half_copies, fixed_copies, field_copies = [], [], []

    def send_half(q):
        half_copies.append(
            send(halves_out.at[q, 1 - h], halves_in.at[q], half_s.at[q], half_g.at[q], c, 1 - h)
        )

    send_half(0)
    for k, peer in enumerate(peers):
        fixed_copies.append(
            send(fixed.at[peer], fixed_in.at[c], fixed_s.at[k], fixed_g.at[k], peer, h)
        )
    fixed_in[c] = fixed[c]
    for q in range(1, BITES):
        project(q)
        send_half(q)
    for q in range(BITES):
        half_copies[q].wait_recv()
        fields[q] = halves_out[q, h] + halves_in[q]
        for k, peer in enumerate(peers):
            field_copies.append(
                send(fields.at[q, peer], fields_in.at[q, c], field_s.at[q, k], field_g.at[q, k], peer, h)
            )
        fields_in[q, c] = fields[q, c]

    mid_real, mid_imag = mid_ref[0], mid_ref[1]

    def gather(rows):
        return jnp.concatenate(
            [
                jnp.concatenate([row[:, s * LANES : (s + 1) * LANES] for row in rows], 1)
                for s in range(splits)
            ],
            0,
        )

    def spread(field, array):
        for i in range(own):
            for s in range(splits):
                back_out[field, :, i, s * LANES : (s + 1) * LANES] = array[
                    s * groups : (s + 1) * groups, i * LANES : (i + 1) * LANES
                ]

    def forward(array):
        stage = exact_dot(t1_ref[...], array)
        rows = []
        for i in range(own):
            real = stage[:coarse, i * LANES : (i + 1) * LANES]
            imag = stage[coarse:, i * LANES : (i + 1) * LANES]
            rows.append(
                jnp.concatenate(
                    [real * mid_real - imag * mid_imag, real * mid_imag + imag * mid_real], 1
                )
            )
        return exact_dot(jnp.concatenate(rows, 0), t2_ref[...])

    def backward(spectrum):
        stage = exact_dot(spectrum, t2i_ref[...])
        blocks = []
        for i in range(own):
            real = stage[i * coarse : (i + 1) * coarse, :LANES]
            imag = stage[i * coarse : (i + 1) * coarse, LANES:]
            blocks.append(
                jnp.concatenate(
                    [real * mid_real + imag * mid_imag, imag * mid_real - real * mid_imag], 0
                )
            )
        return exact_dot(t1i_ref[...], jnp.concatenate(blocks, 1))

    def times(left, right, sign):
        left_real, left_imag = left[:, :LANES], left[:, LANES:]
        right_real, right_imag = right[:, :LANES], sign * right[:, LANES:]
        return jnp.concatenate(
            [
                left_real * right_real - left_imag * right_imag,
                left_real * right_imag + left_imag * right_real,
            ],
            1,
        )

    def field(row):
        return jnp.concatenate([fields_in[q, :, row, :] for q in range(BITES)], 1)

    for copy in fixed_copies:
        copy.wait_recv()
    filters = gather([fixed_in[:, i, :] for i in range(own)])
    targets = gather([fixed_in[:, own + i, :] for i in range(own)])
    skip = jnp.concatenate(
        [jnp.full((1, LANES), skip_ref[c * own + i], jnp.float32) for i in range(own)], 1
    )
    filter_spec = forward(filters)
    for copy in field_copies:
        copy.wait_recv()
    values = gather([field(i) for i in range(own)])
    gates = gather([field(own + i) for i in range(own)])
    value_spec = forward(values)
    conv = backward(times(value_spec, filter_spec, 1.0)) + skip * values
    outputs = gates * conv
    residual = outputs - targets
    grad_conv = residual * gates

    def send_back(f, target):
        return [
            send(back_out.at[f, peer], target, back_s.at[f, k], back_g.at[f, k], peer, h)
            for k, peer in enumerate(peers)
        ]

    def relay(f, copies):
        flows = [send(back_in.at[f, h, c], back_in.at[f, h, c], relay_s.at[f, 0], relay_g.at[f, 0], c, 1 - h)]
        for k, source in enumerate(sources):
            copies[k].wait_recv()
            place = back_in.at[f, h, source]
            flows.append(send(place, place, relay_s.at[f, k + 1], relay_g.at[f, k + 1], c, 1 - h))
        return flows

    spread(1, residual * conv)
    back_in[1, h, c] = back_out[1, c]
    gate_copies = send_back(1, back_in.at[1, h, c])
    spread(2, outputs)
    grad_spec = forward(grad_conv)
    spread(0, backward(times(grad_spec, filter_spec, -1.0)) + skip * grad_conv)
    back_in[0, h, c] = back_out[0, c]
    value_copies = send_back(0, back_in.at[0, h, c])
    late = send_back(2, outputs_ref.at[c])
    flows = relay(1, gate_copies)
    spread(3, backward(times(grad_spec, value_spec, -1.0)) * scaling)
    flows += relay(0, value_copies)
    late += send_back(3, filter_ref.at[c])
    outputs_ref[c] = back_out[2, c]
    filter_ref[c] = back_out[3, c]
    for copy in flows:
        copy.wait_recv()

    for p in range(2):
        for k in range(2 * groups):
            base = p * channels + k * own
            pair_ref[base : base + own, :] = back_in[p, k // groups, k % groups]
    high, low = split(pair_ref[...])
    width = columns // PIECES
    cuts = [pl.ds(j * width, width) for j in range(PIECES)]
    first, second, third = [], [], []
    for j, cut in enumerate(cuts):
        piece = x_ref[:, cut]
        product_rows = jnp.dot(high, piece, preferred_element_type=jnp.float32) + jnp.dot(
            low, piece, preferred_element_type=jnp.float32
        )
        part[..., cut] = product_rows.reshape(part.shape[:-1] + (width,))
        first.append(
            send(part.at[:, :, 1 - core, :, cut], in1.at[:, :, :, cut], s1.at[j], g1.at[j], core_peer, h)
        )
    for j, cut in enumerate(cuts):
        first[j].wait_recv()
        sum1[:, :, :, cut] = part[:, :, core, :, cut] + in1[:, :, :, cut]
        second.append(
            send(sum1.at[:, 1 - x_side, :, cut], in2.at[:, :, cut], s2.at[j], g2.at[j], x_peer, h)
        )
    for j, cut in enumerate(cuts):
        second[j].wait_recv()
        sum2[:, :, cut] = sum1[:, x_side, :, cut] + in2[:, :, cut]
        third.append(
            [
                send(
                    sum2.at[peer // 4, :, cut], in3.at[d, :, cut], s3.at[j, d], g3.at[j, d], peer, h
                )
                for d, peer in enumerate(z_peers)
            ]
        )
    for j, cut in enumerate(cuts):
        total = sum2[z, :, cut]
        for d in range(far - 1):
            third[j][d].wait_recv()
            total = total + in3[d, :, cut]
        proj_ref[:, cut] = total * scaling
    for copy in late:
        copy.wait_recv()
    for copy in sent:
        copy.wait_send()


def final_kernel(
    pair_ref, w_ref, outs_ref, filt_ref, proj_ref, grad_ref, outputs_ref, filter_ref, grad_proj_ref, high, low
):
    groups, own, _ = outs_ref.shape

    @pl.when(pl.program_id(0) == 0)
    def _():
        high[...], low[...] = split(pair_ref[...].T)
        grad_proj_ref[...] = proj_ref[...]
        for g in range(groups):
            outputs_ref[g * own : (g + 1) * own, :] = outs_ref[g]
            filter_ref[g * own : (g + 1) * own, :] = filt_ref[g]

    w = jnp.concatenate([w_ref[0], w_ref[1]], 1)
    flip = (((1,), (1,)), ((), ()))
    grad_ref[...] = lax.dot_general(
        high[...], w, flip, preferred_element_type=jnp.float32
    ) + lax.dot_general(low[...], w, flip, preferred_element_type=jnp.float32)


def per_device(inputs, proj_weight, filters, skip_gain, targets):
    groups, halves = lax.axis_size("ctx"), lax.axis_size("ch")
    frames, columns = inputs.shape
    channels = proj_weight.shape[2]
    own = channels // (groups * halves)
    fits = own * groups * halves == channels and own == 4 and groups % 8 == 0 and halves == 2
    if not fits or frames % (LANES * BITES) or columns % (LANES * PIECES):
        return general(inputs, proj_weight, filters, skip_gain, targets)
    length = frames * groups
    scaling = float(length) ** -0.5
    splits = frames // LANES
    t1, mid, t2, t2i, t1i = spectrum_tables(length // LANES, LANES)
    order = np.arange(length // LANES).reshape(groups, splits).T.reshape(-1)
    f32 = jnp.float32
    tables = [jnp.asarray(table, f32) for table in (t1[:, order], mid, t2, t2i, t1i[order])]
    rows = 2 * channels // groups
    far = groups // 4
    vmem, dma = pltpu.VMEM, pltpu.SemaphoreType.DMA
    bite = frames // BITES
    blocks = jax.ShapeDtypeStruct((groups, own, frames), f32)
    outs, filt, pair, proj = pl.pallas_call(
        functools.partial(main_kernel, own, scaling),
        out_shape=(
            blocks,
            blocks,
            jax.ShapeDtypeStruct((2 * channels, frames), f32),
            jax.ShapeDtypeStruct((rows, columns), f32),
        ),
        in_specs=[VMEM_SPEC] * 4 + [pl.BlockSpec(memory_space=pltpu.SMEM)] + [VMEM_SPEC] * 5,
        out_specs=(VMEM_SPEC,) * 4,
        scratch_shapes=[
            vmem((groups, 2 * own, frames), f32),
            vmem((groups, 2 * own, frames), f32),
            vmem((BITES, 2, groups, 2 * own, bite), f32),
            vmem((BITES, groups, 2 * own, bite), f32),
            vmem((BITES, groups, 2 * own, bite), f32),
            vmem((BITES, groups, 2 * own, bite), f32),
            vmem((4, groups, own, frames), f32),
            vmem((2, 2, groups, own, frames), f32),
            vmem((far, 2, 2, rows, columns), f32),
            vmem((far, 2, rows, columns), f32),
            vmem((far, 2, rows, columns), f32),
            vmem((far, rows, columns), f32),
            vmem((far, rows, columns), f32),
            vmem((far - 1, rows, columns), f32),
            dma((groups - 1,)),
            dma((groups - 1,)),
            dma((BITES,)),
            dma((BITES,)),
            dma((BITES, groups - 1)),
            dma((BITES, groups - 1)),
            dma((4, groups - 1)),
            dma((4, groups - 1)),
            dma((2, groups)),
            dma((2, groups)),
            dma((PIECES,)),
            dma((PIECES,)),
            dma((PIECES,)),
            dma((PIECES,)),
            dma((PIECES, far - 1)),
            dma((PIECES, far - 1)),
        ],
        compiler_params=pltpu.CompilerParams(
            collective_id=0, has_side_effects=True, vmem_limit_bytes=60 * 1024 * 1024
        ),
    )(inputs, proj_weight, filters, targets, skip_gain, *tables)

    def whole(*shape):
        return pl.BlockSpec(shape, lambda j: (0,) * len(shape))

    width = columns // 4
    grad_inputs, outputs, grad_filter, grad_proj = pl.pallas_call(
        final_kernel,
        grid=(4,),
        out_shape=(
            jax.ShapeDtypeStruct((frames, columns), f32),
            jax.ShapeDtypeStruct(filters.shape, f32),
            jax.ShapeDtypeStruct(filters.shape, f32),
            jax.ShapeDtypeStruct((rows, columns), f32),
        ),
        in_specs=[
            whole(2 * channels, frames),
            pl.BlockSpec((2, width, channels), lambda j: (0, j, 0)),
            whole(groups, own, frames),
            whole(groups, own, frames),
            whole(rows, columns),
        ],
        out_specs=(
            pl.BlockSpec((frames, width), lambda j: (0, j)),
            whole(*filters.shape),
            whole(*filters.shape),
            whole(rows, columns),
        ),
        scratch_shapes=[vmem((frames, 2 * channels), jnp.bfloat16)] * 2,
    )(pair, proj_weight, outs, filt, proj)
    return outputs, grad_inputs, grad_filter, grad_proj


def solution(mesh):
    placed = (P("ctx", "ch"), P(None, "ch", None), P("ch", "ctx"), P("ch"), P("ch", "ctx"))
    return jax.shard_map(
        per_device,
        mesh=mesh,
        in_specs=placed,
        out_specs=(P("ch", "ctx"), P("ctx", "ch"), P("ch", "ctx"), P("ctx", "ch")),
        check_vma=False,
    )
```

profile of v0, /device:TPU:0, one launch (start us, length us, event | category | flops | bytes accessed | tf_op | source)
XLA Modules:
  0.0 66.7 jit_solution(1075314501058175837)
XLA Ops:
  0.6 60.8 %shard_map.129 = (f32[16,4,512]{2,1,0:T(4,128)}, f32[16,4,512]{2,1,0:T(4,128)}, f32[256,512]{1,0:T(8,128)}, f32[16,2048]{1,0:T(8,128)}) custom-call(bf16[512,2048]{1,0:T(8,128)(2,1)} %x_ref.1, bf16[2,2048,128]{2,1,0:T(8,128)(2,1)} %w_ref.3, f32[64,512]{1,0:T(8,128)} %filters_ref.1, f32[64,512]{1,0:T(8,128)} %targets_ref.1, f32[64]{0:T(128)} %skip_ref.1, ...), custom_call_target="tpu_custom_call" | custom-call | tf_op jit(solution)/shard_map/pallas_call | solution.py:498
  61.4 5.3 %shard_map.130 = (f32[512,2048]{1,0:T(8,128)}, f32[64,512]{1,0:T(8,128)}, f32[64,512]{1,0:T(8,128)}, f32[16,2048]{1,0:T(8,128)}) custom-call(f32[256,512]{1,0:T(8,128)} %get-tuple-element.12.pair_ref, bf16[2,2048,128]{2,1,0:T(8,128)(2,1)} %w_ref.3, f32[16,4,512]{2,1,0:T(4,128)} %get-tuple-element.13.outs_ref, f32[16,4,512]{2,1,0:T(4,128)} %get-tuple-element.14.filt_ref, ...), custom_call_target="tpu_custom_call" | custom-call | tf_op jit(solution)/shard_map/pallas_call | solution.py:549
where the time goes:
time: 66.9 us; the launch traced here: 66.7 us
  Pallas kernels  66.1 us (99%)
    pallas_call x1, Pallas kernels, per_device(): pl.pallas_call(functools.partial(main_kernel, own, scaling), out_shape=(b...  60.8 us
    pallas_call x1, Pallas kernels, per_device(): pl.pallas_call(final_kernel, grid=(4,), out_shape=(jax.ShapeDtypeStruct((...  5.32 us

commit v1 on v0

--- a/solution.py
+++ b/solution.py
@@ -187,13 +187,9 @@
 
 MESH = pl.DeviceIdType.MESH
 LANES = 128
-PIECES = 8
+PIECES = 4
 BITES = 2
 VMEM_SPEC = pl.BlockSpec(memory_space=pltpu.VMEM)
-
-
-def exact_dot(left, right):
-    return jnp.dot(left, right, precision=HIGHEST, preferred_element_type=jnp.float32)
 
 
 def spectrum_tables(coarse, fine):
@@ -217,21 +213,44 @@
     return high, (array - high.astype(jnp.float32)).astype(jnp.bfloat16)
 
 
+def left_table(table_ref, array):
+    high, low = split(array)
+    return (
+        jnp.dot(table_ref[0], high, preferred_element_type=jnp.float32)
+        + jnp.dot(table_ref[0], low, preferred_element_type=jnp.float32)
+        + jnp.dot(table_ref[1], high, preferred_element_type=jnp.float32)
+    )
+
+
+def right_table(array, table_ref):
+    high, low = split(array)
+    return (
+        jnp.dot(high, table_ref[0], preferred_element_type=jnp.float32)
+        + jnp.dot(low, table_ref[0], preferred_element_type=jnp.float32)
+        + jnp.dot(high, table_ref[1], preferred_element_type=jnp.float32)
+    )
+
+
+def halves_of(table):
+    high = np.asarray(table, jnp.bfloat16)
+    low = np.asarray(table - np.asarray(high, np.float64), jnp.bfloat16)
+    return jnp.asarray(np.stack([high, low]))
+
+
 def main_kernel(
     own, scaling,
     x_ref, w_ref, filters_ref, targets_ref, skip_ref, t1_ref, mid_ref, t2_ref, t2i_ref, t1i_ref,
-    outputs_ref, filter_ref, pair_ref, proj_ref,
+    outputs_ref, filter_ref, high_ref, low_ref, proj_ref,
     fixed, fixed_in, halves_out, halves_in, fields, fields_in, back_out, back_in,
-    part, in1, sum1, in2, sum2, in3,
+    pair, part, in1, sum1, in2, sum2, in3,
     fixed_s, fixed_g, half_s, half_g, field_s, field_g, back_s, back_g, relay_s, relay_g,
     s1, g1, s2, g2, s3, g3,
 ):
-    groups, frames = fixed.shape[0], fixed.shape[2]
+    groups, frames = fixed.shape[1], fixed.shape[3]
     columns = x_ref.shape[1]
     splits = frames // LANES
     coarse = groups * splits
     bite = frames // BITES
-    channels = 2 * groups * own
     far = groups // 4
     c, h = lax.axis_index("ctx"), lax.axis_index("ch")
     core, x_side, z = lax.rem(c, 2), lax.rem(c // 2, 2), c // 4
@@ -261,8 +280,19 @@
     pl.semaphore_signal(barrier, inc=1, device_id=(c, 1 - h), device_id_type=MESH)
 
     for g in range(groups):
-        fixed[g, :own, :] = filters_ref[g * own : (g + 1) * own, :]
-        fixed[g, own:, :] = targets_ref[g * own : (g + 1) * own, :]
+        fixed[0, g] = filters_ref[g * own : (g + 1) * own, :]
+        fixed[1, g] = targets_ref[g * own : (g + 1) * own, :]
+    fixed_copies, half_copies, field_copies = [[], []], [], []
+
+    def send_fixed(f):
+        for k, peer in enumerate(peers):
+            fixed_copies[f].append(
+                send(fixed.at[f, peer], fixed_in.at[f, c], fixed_s.at[f, k], fixed_g.at[f, k], peer, h)
+            )
+        fixed_in[f, c] = fixed[f, c]
+
+    pl.semaphore_wait(barrier, groups)
+    send_fixed(0)
 
     def project(q):
         for p in range(2):
@@ -275,8 +305,6 @@
                 ]
 
     project(0)
-    pl.semaphore_wait(barrier, groups)
-    half_copies, fixed_copies, field_copies = [], [], []
 
     def send_half(q):
         half_copies.append(
@@ -284,11 +312,6 @@
         )
 
     send_half(0)
-    for k, peer in enumerate(peers):
-        fixed_copies.append(
-            send(fixed.at[peer], fixed_in.at[c], fixed_s.at[k], fixed_g.at[k], peer, h)
-        )
-    fixed_in[c] = fixed[c]
     for q in range(1, BITES):
         project(q)
         send_half(q)
@@ -300,6 +323,7 @@
                 send(fields.at[q, peer], fields_in.at[q, c], field_s.at[q, k], field_g.at[q, k], peer, h)
             )
         fields_in[q, c] = fields[q, c]
+    send_fixed(1)
 
     mid_real, mid_imag = mid_ref[0], mid_ref[1]
 
@@ -320,7 +344,7 @@
                 ]
 
     def forward(array):
-        stage = exact_dot(t1_ref[...], array)
+        stage = left_table(t1_ref, array)
         rows = []
         for i in range(own):
             real = stage[:coarse, i * LANES : (i + 1) * LANES]
@@ -330,10 +354,10 @@
                     [real * mid_real - imag * mid_imag, real * mid_imag + imag * mid_real], 1
                 )
             )
-        return exact_dot(jnp.concatenate(rows, 0), t2_ref[...])
+        return right_table(jnp.concatenate(rows, 0), t2_ref)
 
     def backward(spectrum):
-        stage = exact_dot(spectrum, t2i_ref[...])
+        stage = right_table(spectrum, t2i_ref)
         blocks = []
         for i in range(own):
             real = stage[i * coarse : (i + 1) * coarse, :LANES]
@@ -343,7 +367,7 @@
                     [real * mid_real + imag * mid_imag, imag * mid_real - real * mid_imag], 0
                 )
             )
-        return exact_dot(t1i_ref[...], jnp.concatenate(blocks, 1))
+        return left_table(t1i_ref, jnp.concatenate(blocks, 1))
 
     def times(left, right, sign):
         left_real, left_imag = left[:, :LANES], left[:, LANES:]
@@ -359,10 +383,9 @@
     def field(row):
         return jnp.concatenate([fields_in[q, :, row, :] for q in range(BITES)], 1)
 
-    for copy in fixed_copies:
+    for copy in fixed_copies[0]:
         copy.wait_recv()
-    filters = gather([fixed_in[:, i, :] for i in range(own)])
-    targets = gather([fixed_in[:, own + i, :] for i in range(own)])
+    filters = gather([fixed_in[0, :, i, :] for i in range(own)])
     skip = jnp.concatenate(
         [jnp.full((1, LANES), skip_ref[c * own + i], jnp.float32) for i in range(own)], 1
     )
@@ -374,6 +397,9 @@
     value_spec = forward(values)
     conv = backward(times(value_spec, filter_spec, 1.0)) + skip * values
     outputs = gates * conv
+    for copy in fixed_copies[1]:
+        copy.wait_recv()
+    targets = gather([fixed_in[1, :, i, :] for i in range(own)])
     residual = outputs - targets
     grad_conv = residual * gates
 
@@ -402,53 +428,86 @@
     late = send_back(2, outputs_ref.at[c])
     flows = relay(1, gate_copies)
     spread(3, backward(times(grad_spec, value_spec, -1.0)) * scaling)
-    flows += relay(0, value_copies)
+    value_flows = relay(0, value_copies)
     late += send_back(3, filter_ref.at[c])
     outputs_ref[c] = back_out[2, c]
     filter_ref[c] = back_out[3, c]
-    for copy in flows:
-        copy.wait_recv()
-
-    for p in range(2):
-        for k in range(2 * groups):
-            base = p * channels + k * own
-            pair_ref[base : base + own, :] = back_in[p, k // groups, k % groups]
-    high, low = split(pair_ref[...])
+
     width = columns // PIECES
     cuts = [pl.ds(j * width, width) for j in range(PIECES)]
-    first, second, third = [], [], []
-    for j, cut in enumerate(cuts):
-        piece = x_ref[:, cut]
-        product_rows = jnp.dot(high, piece, preferred_element_type=jnp.float32) + jnp.dot(
-            low, piece, preferred_element_type=jnp.float32
-        )
-        part[..., cut] = product_rows.reshape(part.shape[:-1] + (width,))
-        first.append(
-            send(part.at[:, :, 1 - core, :, cut], in1.at[:, :, :, cut], s1.at[j], g1.at[j], core_peer, h)
-        )
-    for j, cut in enumerate(cuts):
-        first[j].wait_recv()
-        sum1[:, :, :, cut] = part[:, :, core, :, cut] + in1[:, :, :, cut]
-        second.append(
-            send(sum1.at[:, 1 - x_side, :, cut], in2.at[:, :, cut], s2.at[j], g2.at[j], x_peer, h)
-        )
-    for j, cut in enumerate(cuts):
-        second[j].wait_recv()
-        sum2[:, :, cut] = sum1[:, x_side, :, cut] + in2[:, :, cut]
-        third.append(
-            [
+    mid_z = far // 2
+    crossings = {}
+
+    def partial_rows(p, arrivals):
+        for copy in arrivals:
+            copy.wait_recv()
+        for k in range(2 * groups):
+            pair[p, k * own : (k + 1) * own, :] = back_in[p, k // groups, k % groups]
+        high, low = split(pair[p])
+        side = slice(p * mid_z, (p + 1) * mid_z)
+        copies = []
+        for j, cut in enumerate(cuts):
+            piece = x_ref[:, cut]
+            product_rows = jnp.dot(high, piece, preferred_element_type=jnp.float32) + jnp.dot(
+                low, piece, preferred_element_type=jnp.float32
+            )
+            part[side, :, :, :, cut] = product_rows.reshape((mid_z,) + part.shape[1:-1] + (width,))
+            span = pl.ds(p * mid_z, mid_z)
+            copies.append(
                 send(
-                    sum2.at[peer // 4, :, cut], in3.at[d, :, cut], s3.at[j, d], g3.at[j, d], peer, h
+                    part.at[span, :, 1 - core, :, cut], in1.at[span, :, :, cut],
+                    s1.at[p, j], g1.at[p, j], core_peer, h,
                 )
-                for d, peer in enumerate(z_peers)
-            ]
-        )
+            )
+        return copies
+
+    def across_x(p, copies):
+        side = slice(p * mid_z, (p + 1) * mid_z)
+        span = pl.ds(p * mid_z, mid_z)
+        onward = []
+        for j, cut in enumerate(cuts):
+            copies[j].wait_recv()
+            sum1[side, :, :, cut] = part[side, :, core, :, cut] + in1[side, :, :, cut]
+            onward.append(
+                send(
+                    sum1.at[span, 1 - x_side, :, cut], in2.at[span, :, cut],
+                    s2.at[p, j], g2.at[p, j], x_peer, h,
+                )
+            )
+        return onward
+
+    def across_z(p, copies):
+        side = slice(p * mid_z, (p + 1) * mid_z)
+        for j, cut in enumerate(cuts):
+            copies[j].wait_recv()
+            sum2[side, :, cut] = sum1[side, x_side, :, cut] + in2[side, :, cut]
+            for d, peer in enumerate(z_peers):
+                place = peer // 4
+                copy = pltpu.make_async_remote_copy(
+                    src_ref=sum2.at[place, :, cut],
+                    dst_ref=in3.at[d, :, cut],
+                    send_sem=s3.at[j, d],
+                    recv_sem=g3.at[j, d],
+                    device_id=(peer, h),
+                    device_id_type=MESH,
+                )
+                crossings[j, d] = copy
+                pl.when(place // mid_z == p)(copy.start)
+
+    gate_first = partial_rows(1, flows)
+    gate_second = across_x(1, gate_first)
+    value_first = partial_rows(0, value_flows)
+    across_z(1, gate_second)
+    value_second = across_x(0, value_first)
+    high_ref[...], low_ref[...] = split(jnp.concatenate([pair[0].T, pair[1].T], 1))
+    across_z(0, value_second)
     for j, cut in enumerate(cuts):
         total = sum2[z, :, cut]
         for d in range(far - 1):
-            third[j][d].wait_recv()
+            crossings[j, d].wait_recv()
             total = total + in3[d, :, cut]
         proj_ref[:, cut] = total * scaling
+    sent.extend(crossings.values())
     for copy in late:
         copy.wait_recv()
     for copy in sent:
@@ -456,13 +515,12 @@
 
 
 def final_kernel(
-    pair_ref, w_ref, outs_ref, filt_ref, proj_ref, grad_ref, outputs_ref, filter_ref, grad_proj_ref, high, low
+    high, low, w_ref, outs_ref, filt_ref, proj_ref, grad_ref, outputs_ref, filter_ref, grad_proj_ref
 ):
     groups, own, _ = outs_ref.shape
 
     @pl.when(pl.program_id(0) == 0)
     def _():
-        high[...], low[...] = split(pair_ref[...].T)
         grad_proj_ref[...] = proj_ref[...]
         for g in range(groups):
             outputs_ref[g * own : (g + 1) * own, :] = outs_ref[g]
@@ -480,7 +538,7 @@
     frames, columns = inputs.shape
     channels = proj_weight.shape[2]
     own = channels // (groups * halves)
-    fits = own * groups * halves == channels and own == 4 and groups % 8 == 0 and halves == 2
+    fits = own * groups * halves == channels and own == 4 and groups % 16 == 0 and halves == 2
     if not fits or frames % (LANES * BITES) or columns % (LANES * PIECES):
         return general(inputs, proj_weight, filters, skip_gain, targets)
     length = frames * groups
@@ -489,39 +547,42 @@
     t1, mid, t2, t2i, t1i = spectrum_tables(length // LANES, LANES)
     order = np.arange(length // LANES).reshape(groups, splits).T.reshape(-1)
     f32 = jnp.float32
-    tables = [jnp.asarray(table, f32) for table in (t1[:, order], mid, t2, t2i, t1i[order])]
+    tables = [halves_of(table) for table in (t1[:, order], t2, t2i, t1i[order])]
+    tables.insert(1, jnp.asarray(mid, f32))
     rows = 2 * channels // groups
     far = groups // 4
     vmem, dma = pltpu.VMEM, pltpu.SemaphoreType.DMA
     bite = frames // BITES
     blocks = jax.ShapeDtypeStruct((groups, own, frames), f32)
-    outs, filt, pair, proj = pl.pallas_call(
+    outs, filt, high, low, proj = pl.pallas_call(
         functools.partial(main_kernel, own, scaling),
         out_shape=(
             blocks,
             blocks,
-            jax.ShapeDtypeStruct((2 * channels, frames), f32),
+            jax.ShapeDtypeStruct((frames, 2 * channels), jnp.bfloat16),
+            jax.ShapeDtypeStruct((frames, 2 * channels), jnp.bfloat16),
             jax.ShapeDtypeStruct((rows, columns), f32),
         ),
         in_specs=[VMEM_SPEC] * 4 + [pl.BlockSpec(memory_space=pltpu.SMEM)] + [VMEM_SPEC] * 5,
-        out_specs=(VMEM_SPEC,) * 4,
+        out_specs=(VMEM_SPEC,) * 5,
         scratch_shapes=[
-            vmem((groups, 2 * own, frames), f32),
-            vmem((groups, 2 * own, frames), f32),
+            vmem((2, groups, own, frames), f32),
+            vmem((2, groups, own, frames), f32),
             vmem((BITES, 2, groups, 2 * own, bite), f32),
             vmem((BITES, groups, 2 * own, bite), f32),
             vmem((BITES, groups, 2 * own, bite), f32),
             vmem((BITES, groups, 2 * own, bite), f32),
             vmem((4, groups, own, frames), f32),
             vmem((2, 2, groups, own, frames), f32),
+            vmem((2, channels, frames), f32),
             vmem((far, 2, 2, rows, columns), f32),
             vmem((far, 2, rows, columns), f32),
             vmem((far, 2, rows, columns), f32),
             vmem((far, rows, columns), f32),
             vmem((far, rows, columns), f32),
             vmem((far - 1, rows, columns), f32),
-            dma((groups - 1,)),
-            dma((groups - 1,)),
+            dma((2, groups - 1)),
+            dma((2, groups - 1)),
             dma((BITES,)),
             dma((BITES,)),
             dma((BITES, groups - 1)),
@@ -530,10 +591,10 @@
             dma((4, groups - 1)),
             dma((2, groups)),
             dma((2, groups)),
-            dma((PIECES,)),
-            dma((PIECES,)),
-            dma((PIECES,)),
-            dma((PIECES,)),
+            dma((2, PIECES)),
+            dma((2, PIECES)),
+            dma((2, PIECES)),
+            dma((2, PIECES)),
             dma((PIECES, far - 1)),
             dma((PIECES, far - 1)),
         ],
@@ -556,7 +617,8 @@
             jax.ShapeDtypeStruct((rows, columns), f32),
         ),
         in_specs=[
-            whole(2 * channels, frames),
+            whole(frames, 2 * channels),
+            whole(frames, 2 * channels),
             pl.BlockSpec((2, width, channels), lambda j: (0, j, 0)),
             whole(groups, own, frames),
             whole(groups, own, frames),
@@ -568,8 +630,7 @@
             whole(*filters.shape),
             whole(rows, columns),
         ),
-        scratch_shapes=[vmem((frames, 2 * channels), jnp.bfloat16)] * 2,
-    )(pair, proj_weight, outs, filt, proj)
+    )(high, low, proj_weight, outs, filt, proj)
     return outputs, grad_inputs, grad_filter, grad_proj
 
 

time: 66.9 us -> 69.3 us (1.036)
  Pallas kernels: 66.1 us -> 68.5 us
    pallas_call x1, Pallas kernels: 60.8 us -> 63.3 us  [per_device(): pl.pallas_call(functools.partial(main_kernel, own, scaling), out_shape=(b...]
where the time goes in v1:
time: 69.3 us; the launch traced here: 69.1 us
  Pallas kernels  68.5 us (99%)
    pallas_call x1, Pallas kernels, per_device(): pl.pallas_call(functools.partial(main_kernel, own, scaling), out_shape=(b...  63.3 us
    pallas_call x1, Pallas kernels, per_device(): pl.pallas_call(final_kernel, grid=(4,), out_shape=(jax.ShapeDtypeStruct((...  5.17 us

profile of v1, /device:TPU:0, one launch (start us, length us, event | category | flops | bytes accessed | tf_op | source)
XLA Modules:
  0.0 69.1 jit_solution(8329199747379574291)
XLA Ops:
  0.6 63.3 %shard_map.129 = (f32[16,4,512]{2,1,0:T(4,128)}, f32[16,4,512]{2,1,0:T(4,128)}, bf16[512,256]{1,0:T(8,128)(2,1)}, bf16[512,256]{1,0:T(8,128)(2,1)}, f32[16,2048]{1,0:T(8,128)}) custom-call(bf16[512,2048]{1,0:T(8,128)(2,1)} %x_ref.1, bf16[2,2048,128]{2,1,0:T(8,128)(2,1)} %w_ref.3, f32[64,512]{1,0:T(8,128)} %filters_ref.1, f32[64,512]{1,0:T(8,128)} %targets_ref.1, ...), custom_call_target="tpu_custom_call" | custom-call | tf_op jit(solution)/shard_map/pallas_call | solution.py:557
  64.0 5.2 %shard_map.130 = (f32[512,2048]{1,0:T(8,128)}, f32[64,512]{1,0:T(8,128)}, f32[64,512]{1,0:T(8,128)}, f32[16,2048]{1,0:T(8,128)}) custom-call(bf16[512,256]{1,0:T(8,128)(2,1)} %get-tuple-element.13.high, bf16[512,256]{1,0:T(8,128)(2,1)} %get-tuple-element.14.low, bf16[2,2048,128]{2,1,0:T(8,128)(2,1)} %w_ref.3, f32[16,4,512]{2,1,0:T(4,128)} %get-tuple-element.15.outs_ref, ...), custom_call_target="tpu_custom_call" | custom-call | tf_op jit(solution)/shard_map/pallas_call | solution.py:610
